TPU v7x, 256 devices: a whole 4x4x8 slice. The times are simulated.
256 devices in a mesh: row: 16 (over y, z_hi, core), col: 16 (over x, z_lo).
Axes of the slice: x: 4, y: 4, z: 8 (z_hi: 2, z_lo: 4; z = z_hi * 4 + z_lo), core: 2. Of those that a mesh axis runs over, the one named last changes fastest.
Arguments:
- eigvec: float32 [16384, 20480], P('row', 'col'), may hold values from -6 to 6
- panels: float32 [3, 16384, 256], P(None, ('row', 'col')), may hold values from -0.375 to 0.375
- factors: float32 [3, 256, 256], replicated, may hold values from -0.046875 to 0.046875
Outputs:
- updated: float32 [16384, 20480], P('row', 'col')
All inputs are finite; a program needn't handle non-finite values.
Results may differ from a plain program's by a relative error of at most 0.00012.
Values sent between devices are 32-bit elements; how exact they have to be, the bound alone decides.
No kernel may reach another device: no remote copies, remote signals or barrier semaphores. Data moves between devices by JAX's collectives and lax.ppermute only.
A program may use at most 64 MiB of HBM per device.

v0:
```python
import jax
import jax.numpy as jnp
from jax import lax
from jax.sharding import PartitionSpec as P

NREF = 3


def per_device(eigvec, panels, factors):
    highest = lax.Precision.HIGHEST
    local_panels = lax.all_gather(panels, "col", axis=1, tiled=True)
    upper = jnp.triu(factors)
    field = eigvec
    for index in range(NREF):
        panel = local_panels[index]
        partial_value = jnp.dot(
            panel.T, field, precision=highest, preferred_element_type=jnp.float32
        )
        coeff = lax.psum(partial_value, "row")
        scaled = jnp.dot(upper[index], coeff, precision=highest, preferred_element_type=jnp.float32)
        field = field - jnp.dot(
            panel, scaled, precision=highest, preferred_element_type=jnp.float32
        )
    return field


def solution(mesh):
    in_specs = (P("row", "col"), P(None, ("row", "col"), None), P())
    out_specs = P("row", "col")
    return jax.shard_map(
        per_device, mesh=mesh, in_specs=in_specs, out_specs=out_specs, check_vma=False
    )
```

profile of v0, /device:TPU:6, one launch (start us, length us, event | category | flops | bytes accessed | tf_op | source)
XLA Modules:
  0.0 732.5 jit_solution(2493736768185251348)
XLA Ops:
  6.5 0.0 all-gather.2.cloned.1.call-start
  6.5 0.7 all-gather.2.cloned.1.call-update
  7.3 0.0 all-reduce.4.cloned.1.call-start
  7.3 91.0 %all-gather.2.cloned.1.call-done = f32[3,1024,256]{2,1,0:T(8,128)} async-done(((f32[3,64,256]{2,1,0:T(8,128)}), f32[3,1024,256]{2,1,0:T(8,128)}) %all-gather.2.cloned.1.call-update) | async-done | bytes 3145744 | tf_op jit(solution)/shard_map/all_gather | solution.py:11
  98.3 8.4 %fusion = f32[256,1280]{1,0:T(8,128)} fusion(f32[1024,1280]{1,0:T(8,128)} %param.3, f32[3,1024,256]{2,1,0:T(8,128)} %all-gather.2.cloned.1.call-done), kind=kOutput, calls=%fused_computation.8 | convolution fusion | flops 4026531840 | bytes 7602176 | tf_op jit(solution)/shard_map/dot_general | solution.py:16
  106.7 0.0 all-reduce.4.cloned.1.call-update
  106.8 0.2 all-reduce.6.cloned.1.call-start
  107.0 5.9 copy.4
  112.9 0.0 copy-start.2
  112.9 0.1 iota_compare_fusion
  113.0 2.3 broadcast_select_fusion
  115.2 177.7 %all-reduce.4.cloned.1.call-done = f32[256,1280]{1,0:T(8,128)} async-done(((f32[256,1280]{1,0:T(8,128)}), f32[256,1280]{1,0:T(8,128)}) %all-reduce.4.cloned.1.call-update) | async-done | bytes 1310736 | tf_op jit(solution)/shard_map/psum | solution.py:19
  293.0 2.6 fusion.3
  295.6 0.0 copy-done.2
  295.6 10.7 %bitcast_subtract_fusion.2 = f32[1024,1280]{0,1:T(8,128)S(1)} fusion(f32[1024,1280]{0,1:T(8,128)} %copy.4, f32[256,1280]{1,0:T(8,128)S(1)} %fusion.3, f32[3,1024,256]{2,1,0:T(8,128)S(1)} %copy-done.2), kind=kOutput, calls=%fused_computation.2 | convolution fusion | flops 4027842560 | bytes 12845056 | tf_op jit(solution)/shard_map/dot_general | solution.py:21
  306.4 0.0 copy-start
  306.4 2.3 copy-done
  308.7 5.4 convolution_bitcast_fusion.1
  314.1 0.0 all-reduce.6.cloned.1.call-update
  314.2 0.3 all-reduce.8.cloned.1.call-start
  314.4 184.6 %all-reduce.6.cloned.1.call-done = f32[256,1280]{0,1:T(8,128)} async-done(((f32[256,1280]{0,1:T(8,128)}), f32[256,1280]{0,1:T(8,128)}) %all-reduce.6.cloned.1.call-update) | async-done | bytes 1310736 | tf_op jit(solution)/shard_map/psum | solution.py:19
  499.0 2.7 fusion.2
  501.7 10.7 %bitcast_subtract_fusion.1 = f32[1024,1280]{0,1:T(8,128)S(1)} fusion(f32[1024,1280]{0,1:T(8,128)} %copy-done, f32[256,1280]{1,0:T(8,128)S(1)} %fusion.2, f32[3,1024,256]{2,1,0:T(8,128)S(1)} %copy-done.2), kind=kOutput, calls=%fused_computation.1 | convolution fusion | flops 4027842560 | bytes 12845056 | tf_op jit(solution)/shard_map/dot_general | solution.py:21
  512.4 0.0 copy-start.1
  512.4 2.3 copy-done.1
  514.8 5.4 convolution_bitcast_fusion
  520.2 0.0 all-reduce.8.cloned.1.call-update
  520.2 184.8 %all-reduce.8.cloned.1.call-done = f32[256,1280]{0,1:T(8,128)} async-done(((f32[256,1280]{0,1:T(8,128)}), f32[256,1280]{0,1:T(8,128)}) %all-reduce.8.cloned.1.call-update) | async-done | bytes 1310736 | tf_op jit(solution)/shard_map/psum | solution.py:19
  705.0 2.7 fusion.1
  707.7 12.4 %bitcast_subtract_fusion = f32[1024,1280]{0,1:T(8,128)} fusion(f32[1024,1280]{0,1:T(8,128)} %copy-done.1, f32[256,1280]{1,0:T(8,128)S(1)} %fusion.1, f32[3,1024,256]{2,1,0:T(8,128)S(1)} %copy-done.2), kind=kOutput, calls=%fused_computation | convolution fusion | flops 4027842560 | bytes 12845056 | tf_op jit(solution)/shard_map/dot_general | solution.py:21
  720.1 5.9 copy.5
  (1 shorter events, 0.0 us)
Async XLA Ops:
  6.5 91.8 %all-gather.2.cloned.1.call-start = ((), (), s32[]{:S(2)}) async-start(), calls=%async_computation | async-start | bytes 3342336 | tf_op jit(solution)/shard_map/all_gather | solution.py:11
  7.3 285.7 %all-reduce.4.cloned.1.call-start = ((), (), s32[]{:S(2)}) async-start(), calls=%async_computation.1 | async-start | bytes 2621440 | tf_op jit(solution)/shard_map/psum | solution.py:19
  106.8 392.3 %all-reduce.6.cloned.1.call-start = ((), (), s32[]{:S(2)}) async-start(), calls=%async_computation.2 | async-start | bytes 2621440 | tf_op jit(solution)/shard_map/psum | solution.py:19
  112.9 182.8 %copy-start.2 = (f32[3,1024,256]{2,1,0:T(8,128)S(1)}, f32[3,1024,256]{2,1,0:T(8,128)}, u32[]{:S(2)}) copy-start(f32[3,1024,256]{2,1,0:T(8,128)} %all-gather.2.cloned.1.call-done) | copy-start | bytes 9437188
  306.4 2.4 copy-start
  314.2 390.8 %all-reduce.8.cloned.1.call-start = ((), (), s32[]{:S(2)}) async-start(), calls=%async_computation.3 | async-start | bytes 2621440 | tf_op jit(solution)/shard_map/psum | solution.py:19
  512.4 2.4 copy-start.1
Sparse Core Ops, SparseCore 0:
  9.1 89.1 all-gather.1
  106.9 186.0 all-reduce.3
  314.3 184.6 all-reduce.5
  520.3 184.6 all-reduce.7
where the time goes:
time: 733 us
  waiting for transfers between devices  639 us (87%)
  matrix products  61.1 us (8%)
  local copies, waits for them, and re-layouts  16.5 us (2%)
  between operations  13.2 us (2%)
    psum x3, waiting for transfers between devices, per_device(): coeff = lax.psum(partial_value, 'row')  547 us
    all_gather x1, waiting for transfers between devices, per_device(): local_panels = lax.all_gather(panels, 'col', axis=1, tiled=True)  91 us
    dot_general x3, matrix products, per_device(): jnp.dot(panel, scaled, precision=highest, preferred_element_type=jnp.floa...  33.9 us
    dot_general x3, matrix products, per_device(): jnp.dot(panel.T, field, precision=highest, preferred_element_type=jnp.flo...  19.2 us
  transfers between devices with their start and end apart: 4, of which 4 were waited for; matrix products, arithmetic and copies ran while one was open for 1% of the time, Pallas kernels for 0%

commit v1 on v0

--- a/solution.py
+++ b/solution.py
@@ -2,13 +2,17 @@
 import jax.numpy as jnp
 from jax import lax
 from jax.sharding import PartitionSpec as P
+from jax.lax import all_to_all, axis_size
 
 NREF = 3
 
 
 def per_device(eigvec, panels, factors):
     highest = lax.Precision.HIGHEST
-    local_panels = lax.all_gather(panels, "col", axis=1, tiled=True)
+    _convert_leaves = lambda row_data, ax_name: jnp.concatenate(
+        all_to_all(jnp.stack([row_data] * axis_size(ax_name)), ax_name, 0, 0), axis=1
+    )
+    local_panels = _convert_leaves(panels, "col")
     upper = jnp.triu(factors)
     field = eigvec
     for index in range(NREF):

time: 733 us -> 717 us (0.978)
  waiting for transfers between devices: 639 us -> 545 us
  blocking collectives: 0 us -> 79.2 us
    all_gather x1 -> x0, waiting for transfers between devices: 91 us -> none  [per_device(): local_panels = lax.all_gather(panels, 'col', axis=1, tiled=True)]
    all_to_all x0 -> x1, blocking collectives: none -> 79.2 us  [per_device(): all_to_all(jnp.stack([row_data] * axis_size(ax_name)), ax_name, 0, 0)]
  transfers between devices with their start and end apart: 4 -> 3, of which waited for: 4 -> 3; matrix products, arithmetic and copies ran while one was open for 1% -> 1% of each run, Pallas kernels for 0% -> 0%
where the time goes in v1:
time: 717 us; the launch traced here: 716 us
  waiting for transfers between devices  545 us (76%)
  blocking collectives  79.2 us (11%)
  matrix products  58.2 us (8%)
  local copies, waits for them, and re-layouts  18.1 us (3%)
  between operations  13.2 us (2%)
    psum x3, waiting for transfers between devices, per_device(): coeff = lax.psum(partial_value, 'row')  545 us
    all_to_all x1, blocking collectives, per_device(): all_to_all(jnp.stack([row_data] * axis_size(ax_name)), ax_name, 0, 0)  79.2 us
    dot_general x3, matrix products, per_device(): jnp.dot(panel, scaled, precision=highest, preferred_element_type=jnp.floa...  33.9 us
    dot_general x3, matrix products, per_device(): jnp.dot(panel.T, field, precision=highest, preferred_element_type=jnp.flo...  16.5 us
  transfers between devices with their start and end apart: 3, of which 3 were waited for; matrix products, arithmetic and copies ran while one was open for 1% of the time, Pallas kernels for 0%

profile of v1, /device:TPU:6, one launch (start us, length us, event | category | flops | bytes accessed | tf_op | source)
XLA Modules:
  0.0 716.1 jit_solution(10189440810145416343)
XLA Ops:
  6.5 0.0 all-reduce.4.cloned.1.call-start
  6.5 1.4 stack.2
  8.0 0.0 slice-start.1
  8.0 79.2 %all_to_all.5 = f32[16,3,64,256]{3,2,1,0:T(8,128)S(1)} all-to-all(f32[16,3,64,256]{3,2,1,0:T(8,128)S(1)} %stack.2), channel_id=1, replica_groups=mesh['row'=16,'col'=16] {'col'}, dimensions={0} | all-to-all | bytes 6291456 | tf_op jit(solution)/shard_map/all_to_all | solution.py:13
  87.2 0.2 fusion.3
  87.4 0.0 slice-done
  87.4 0.0 slice-done.1
  87.4 5.7 fusion.4
  93.1 0.0 all-reduce.4.cloned.1.call-update
  93.2 0.2 all-reduce.6.cloned.1.call-start
  93.4 5.9 copy.4
  99.3 0.1 iota_compare_fusion
  99.4 2.1 broadcast_select_fusion
  101.5 175.7 %all-reduce.4.cloned.1.call-done = f32[256,1280]{1,0:T(8,128)} async-done(((f32[256,1280]{1,0:T(8,128)}), f32[256,1280]{1,0:T(8,128)}) %all-reduce.4.cloned.1.call-update) | async-done | bytes 1310736 | tf_op jit(solution)/shard_map/psum | solution.py:23
  277.2 2.7 fusion.2
  279.9 10.7 %bitcast_subtract_fusion.2 = f32[1024,1280]{0,1:T(8,128)S(1)} fusion(f32[1024,1280]{0,1:T(8,128)} %copy.4, f32[256,1280]{1,0:T(8,128)S(1)} %fusion.2, f32[1024,256]{1,0:T(8,128)S(1)} %bitcast.46), kind=kOutput, calls=%fused_computation.2 | convolution fusion | flops 4027842560 | bytes 12845056 | tf_op jit(solution)/shard_map/dot_general | solution.py:25
  290.6 0.0 copy-start
  290.7 2.3 copy-done
  293.0 5.4 convolution_bitcast_fusion.1
  298.4 0.0 all-reduce.6.cloned.1.call-update
  298.4 0.3 all-reduce.8.cloned.1.call-start
  298.7 184.5 %all-reduce.6.cloned.1.call-done = f32[256,1280]{0,1:T(8,128)} async-done(((f32[256,1280]{0,1:T(8,128)}), f32[256,1280]{0,1:T(8,128)}) %all-reduce.6.cloned.1.call-update) | async-done | bytes 1310736 | tf_op jit(solution)/shard_map/psum | solution.py:23
  483.2 2.6 fusion.1
  485.7 10.7 %bitcast_subtract_fusion.1 = f32[1024,1280]{0,1:T(8,128)S(1)} fusion(f32[1024,1280]{0,1:T(8,128)} %copy-done, f32[256,1280]{1,0:T(8,128)S(1)} %fusion.1, f32[1024,256]{1,0:T(8,128)S(1)} %bitcast.44), kind=kOutput, calls=%fused_computation.1 | convolution fusion | flops 4027842560 | bytes 12845056 | tf_op jit(solution)/shard_map/dot_general | solution.py:25
  496.5 0.0 copy-start.1
  496.5 2.3 copy-done.1
  498.9 5.4 convolution_bitcast_fusion
  504.2 0.0 all-reduce.8.cloned.1.call-update
  504.3 184.4 %all-reduce.8.cloned.1.call-done = f32[256,1280]{0,1:T(8,128)} async-done(((f32[256,1280]{0,1:T(8,128)}), f32[256,1280]{0,1:T(8,128)}) %all-reduce.8.cloned.1.call-update) | async-done | bytes 1310736 | tf_op jit(solution)/shard_map/psum | solution.py:23
  688.7 2.6 fusion
  691.3 12.4 %bitcast_subtract_fusion = f32[1024,1280]{0,1:T(8,128)} fusion(f32[1024,1280]{0,1:T(8,128)} %copy-done.1, f32[256,1280]{1,0:T(8,128)S(1)} %fusion, f32[1024,256]{1,0:T(8,128)S(1)} %bitcast.42), kind=kOutput, calls=%fused_computation | convolution fusion | flops 4027842560 | bytes 12845056 | tf_op jit(solution)/shard_map/dot_general | solution.py:25
  703.7 5.9 copy.5
  (5 shorter events, 0.0 us)
Async XLA Ops:
  6.5 270.7 %all-reduce.4.cloned.1.call-start = ((), (), s32[]{:S(2)}) async-start(), calls=%async_computation.1 | async-start | bytes 2621440 | tf_op jit(solution)/shard_map/psum | solution.py:23
  6.5 80.8 %slice-start = ((s8[5242880]{0:T(1024)(128)(4,1)}), s8[4194304]{0:T(1024)(128)(4,1)S(1)}, s32[]{:S(2)}) async-start(s8[5242880]{0:T(1024)(128)(4,1)} %bitcast.38), calls=%async_computation.4 | async-start | bytes 8388608
  8.0 79.4 %slice-start.1 = ((s8[5242880]{0:T(1024)(128)(4,1)}), s8[1048576]{0:T(1024)(128)(4,1)S(1)}, s32[]{:S(2)}) async-start(s8[5242880]{0:T(1024)(128)(4,1)} %bitcast.38), calls=%async_computation.5 | async-start | bytes 2097152
  93.2 390.0 %all-reduce.6.cloned.1.call-start = ((), (), s32[]{:S(2)}) async-start(), calls=%async_computation.2 | async-start | bytes 2621440 | tf_op jit(solution)/shard_map/psum | solution.py:23
  290.6 2.4 copy-start
  298.4 184.8 %copy-start.2 = (f32[3,256,256]{2,1,0:T(8,128)S(1)}, f32[3,256,256]{2,1,0:T(8,128)}, u32[]{:S(2)}) copy-start(f32[3,256,256]{2,1,0:T(8,128)} %broadcast_select_fusion) | copy-start | bytes 2359300
  298.4 390.3 %all-reduce.8.cloned.1.call-start = ((), (), s32[]{:S(2)}) async-start(), calls=%async_computation.3 | async-start | bytes 2621440 | tf_op jit(solution)/shard_map/psum | solution.py:23
  496.5 2.4 copy-start.1
Sparse Core Ops, SparseCore 0:
  93.3 183.9 all-reduce.3
  298.5 184.5 all-reduce.5
  504.4 184.2 all-reduce.7

commit v2 on v0

--- a/solution.py
+++ b/solution.py
@@ -4,6 +4,10 @@
 from jax.sharding import PartitionSpec as P
 
 NREF = 3
+
+
+def replace_copies(x_part, peer_axis="row"):
+    return lax.all_gather(x_part, peer_axis).sum(axis=0)
 
 
 def per_device(eigvec, panels, factors):
@@ -16,7 +20,7 @@
         partial_value = jnp.dot(
             panel.T, field, precision=highest, preferred_element_type=jnp.float32
         )
-        coeff = lax.psum(partial_value, "row")
+        coeff = replace_copies(partial_value)
         scaled = jnp.dot(upper[index], coeff, precision=highest, preferred_element_type=jnp.float32)
         field = field - jnp.dot(
             panel, scaled, precision=highest, preferred_element_type=jnp.float32

time: 733 us -> 872 us (1.19)
  waiting for transfers between devices: 639 us -> 726 us
  local copies, waits for them, and re-layouts: 16.5 us -> 43.2 us
  other arithmetic: 2.36 us -> 26.9 us
    all_gather x0 -> x3, waiting for transfers between devices: none -> 634 us  [replace_copies(): return lax.all_gather(x_part, peer_axis).sum(axis=0)]
    psum x3 -> x0, waiting for transfers between devices: 547 us -> none  [per_device(): coeff = lax.psum(partial_value, 'row')]
    unnamed x7 -> x23, local copies, waits for them, and re-layouts: 10.6 us -> 37.3 us
    reduce_sum x0 -> x3, other arithmetic: none -> 25.7 us  [replace_copies(): return lax.all_gather(x_part, peer_axis).sum(axis=0)]
where the time goes in v2:
time: 872 us; the launch traced here: 866 us
  waiting for transfers between devices  726 us (83%)
  matrix products  56 us (6%)
  local copies, waits for them, and re-layouts  43.2 us (5%)
  other arithmetic  26.9 us (3%)
  between operations  13.6 us (2%)
    all_gather x3, waiting for transfers between devices, replace_copies(): return lax.all_gather(x_part, peer_axis).sum(axis=0)  634 us
    all_gather x1, waiting for transfers between devices, per_device(): local_panels = lax.all_gather(panels, 'col', axis=1, tiled=True)  91 us
    unnamed x23, local copies, waits for them, and re-layouts  37.3 us
    dot_general x3, matrix products, per_device(): jnp.dot(panel, scaled, precision=highest, preferred_element_type=jnp.floa...  31.2 us
    reduce_sum x3, other arithmetic, replace_copies(): return lax.all_gather(x_part, peer_axis).sum(axis=0)  25.7 us
    dot_general x3, matrix products, per_device(): jnp.dot(panel.T, field, precision=highest, preferred_element_type=jnp.flo...  19.7 us
  transfers between devices with their start and end apart: 4, of which 4 were waited for; matrix products, arithmetic and copies ran while one was open for 1% of the time, Pallas kernels for 0%

profile of v2, /device:TPU:6, one launch (start us, length us, event | category | flops | bytes accessed | tf_op | source)
XLA Modules:
  0.0 866.1 jit_solution(7801301453817676552)
XLA Ops:
  6.5 0.7 all-gather.8.cloned.1.call-update
  7.3 0.0 all-gather.10.cloned.1.call-start
  7.3 91.0 %all-gather.8.cloned.1.call-done = f32[3,1024,256]{2,1,0:T(8,128)} async-done(((f32[3,64,256]{2,1,0:T(8,128)}), f32[3,1024,256]{2,1,0:T(8,128)}) %all-gather.8.cloned.1.call-update) | async-done | bytes 3145744 | tf_op jit(solution)/shard_map/all_gather | solution.py:15
  98.3 8.5 fusion
  106.8 0.0 all-gather.10.cloned.1.call-update
  106.8 0.0 copy-start.5
  106.8 0.5 all-gather.12.cloned.1.call-start
  107.3 5.9 copy.6
  113.2 0.1 iota_compare_fusion
  113.4 1.0 broadcast_select_fusion
  114.4 202.9 %all-gather.10.cloned.1.call-done = f32[4096,1280]{1,0:T(8,128)} async-done(((f32[256,1280]{1,0:T(8,128)}), f32[4096,1280]{1,0:T(8,128)}) %all-gather.10.cloned.1.call-update) | async-done | bytes 20971536 | tf_op jit(solution)/shard_map/all_gather | solution.py:10
  317.3 9.3 %reduce_sum.27 = f32[256,1280]{1,0:T(8,128)} reduce(f32[16,256,1280]{2,1,0:T(8,128)} %bitcast.55, f32[]{:T(128)} %constant.6.clone.1), dimensions={0}, to_apply=%region_0.1 | reduce | flops 4915200 | bytes 22282244 | tf_op jit(solution)/shard_map/reduce_sum | solution.py:10
  326.6 2.6 fusion.3
  329.3 10.7 %bitcast_subtract_fusion.2 = f32[1024,1280]{0,1:T(8,128)S(1)} fusion(f32[1024,1280]{0,1:T(8,128)} %copy.6, f32[256,1280]{1,0:T(8,128)S(1)} %fusion.3, f32[3,1024,256]{2,1,0:T(8,128)S(1)} %copy-done.2), kind=kOutput, calls=%fused_computation.4 | convolution fusion | flops 4027842560 | bytes 12845056 | tf_op jit(solution)/shard_map/dot_general | solution.py:25
  340.1 2.3 copy-done
  342.4 5.5 convolution_bitcast_fusion.1
  347.9 0.0 all-gather.12.cloned.1.call-update
  347.9 0.2 all-gather.14.cloned.1.call-start
  348.1 215.3 %all-gather.12.cloned.1.call-done = f32[4096,1280]{0,1:T(8,128)} async-done(((f32[256,1280]{0,1:T(8,128)}), f32[4096,1280]{0,1:T(8,128)}) %all-gather.12.cloned.1.call-update) | async-done | bytes 20971536 | tf_op jit(solution)/shard_map/all_gather | solution.py:10
  563.4 13.4 %copy.8 = f32[160,8,16,256]{3,2,1,0:T(8,128)S(1)} copy(f32[160,8,16,256]{3,1,2,0:T(8,128)} %bitcast.56) | data formatting | bytes 41943040
  576.8 8.2 bitcast_reduce_fusion.1
  585.0 1.3 fusion.2
  586.3 8.7 %bitcast_subtract_fusion.1 = f32[1024,1280]{0,1:T(8,128)S(1)} fusion(f32[1024,1280]{0,1:T(8,128)S(1)} %bitcast.52, f32[256,1280]{1,0:T(8,128)S(1)} %fusion.2, f32[3,1024,256]{2,1,0:T(8,128)S(1)} %copy-done.3), kind=kOutput, calls=%fused_computation.3 | convolution fusion | flops 4027842560 | bytes 12845056 | tf_op jit(solution)/shard_map/dot_general | solution.py:25
  595.1 2.3 copy-done.1
  597.5 5.7 convolution_bitcast_fusion
  603.2 0.0 all-gather.14.cloned.1.call-update
  603.2 215.7 %all-gather.14.cloned.1.call-done = f32[4096,1280]{0,1:T(8,128)} async-done(((f32[256,1280]{0,1:T(8,128)}), f32[4096,1280]{0,1:T(8,128)}) %all-gather.14.cloned.1.call-update) | async-done | bytes 20971536 | tf_op jit(solution)/shard_map/all_gather | solution.py:10
  818.9 13.4 %copy.9 = f32[160,8,16,256]{3,2,1,0:T(8,128)S(1)} copy(f32[160,8,16,256]{3,1,2,0:T(8,128)} %bitcast.57) | data formatting | bytes 41943040
  832.3 8.2 bitcast_reduce_fusion
  840.5 1.3 fusion.1
  841.8 11.7 %bitcast_subtract_fusion = f32[1024,1280]{0,1:T(8,128)} fusion(f32[1024,1280]{0,1:T(8,128)S(1)} %bitcast.54, f32[256,1280]{1,0:T(8,128)S(1)} %fusion.1, f32[3,1024,256]{2,1,0:T(8,128)} %all-gather.8.cloned.1.call-done), kind=kOutput, calls=%fused_computation.2 | convolution fusion | flops 4027842560 | bytes 12845056 | tf_op jit(solution)/shard_map/dot_general | solution.py:25
  853.5 5.9 copy.7
  (21 shorter events, 0.0 us)
Async XLA Ops:
  6.5 91.8 %all-gather.8.cloned.1.call-start = ((), (), s32[]{:S(2)}) async-start(), calls=%async_computation | async-start | bytes 3342336 | tf_op jit(solution)/shard_map/all_gather | solution.py:15
  7.3 310.0 %all-gather.10.cloned.1.call-start = ((), (), s32[]{:S(2)}) async-start(), calls=%async_computation.1 | async-start | bytes 22282240 | tf_op jit(solution)/shard_map/all_gather | solution.py:10
  106.8 6.5 copy-start.5
  106.8 456.6 %all-gather.12.cloned.1.call-start = ((), (), s32[]{:S(2)}) async-start(), calls=%async_computation.2 | async-start | bytes 22282240 | tf_op jit(solution)/shard_map/all_gather | solution.py:10
  317.3 12.0 %copy-start.2 = (f32[3,1024,256]{2,1,0:T(8,128)S(1)}, f32[3,1024,256]{2,1,0:T(8,128)}, u32[]{:S(2)}) copy-start(f32[3,1024,256]{2,1,0:T(8,128)} %all-gather.8.cloned.1.call-done) | copy-start | bytes 9437188
  340.0 2.4 copy-start
  347.9 238.4 %slice-start = ((s8[5242880]{0:T(1024)(128)(4,1)}), s8[1048576]{0:T(1024)(128)(4,1)S(1)}, s32[]{:S(2)}) async-start(s8[5242880]{0:T(1024)(128)(4,1)} %bitcast.51), calls=%async_computation.4 | async-start | bytes 2097152
  347.9 471.0 %all-gather.14.cloned.1.call-start = ((), (), s32[]{:S(2)}) async-start(), calls=%async_computation.3 | async-start | bytes 22282240 | tf_op jit(solution)/shard_map/all_gather | solution.py:10
  563.4 22.9 %slice-start.1 = ((s8[5242880]{0:T(1024)(128)(4,1)}), s8[4194304]{0:T(1024)(128)(4,1)S(1)}, s32[]{:S(2)}) async-start(s8[5242880]{0:T(1024)(128)(4,1)} %bitcast.51), calls=%async_computation.5 | async-start | bytes 8388608
  576.8 8.2 copy-start.4
  576.8 9.5 %copy-start.3 = (f32[3,1024,256]{2,1,0:T(8,128)S(1)}, f32[3,1024,256]{2,1,0:T(8,128)}, u32[]{:S(2)}) copy-start(f32[3,1024,256]{2,1,0:T(8,128)} %all-gather.8.cloned.1.call-done) | copy-start | bytes 9437188
  595.1 2.4 copy-start.1
  603.2 238.6 %slice-start.2 = ((s8[5242880]{0:T(1024)(128)(4,1)}), s8[1048576]{0:T(1024)(128)(4,1)S(1)}, s32[]{:S(2)}) async-start(s8[5242880]{0:T(1024)(128)(4,1)} %bitcast.53), calls=%async_computation.6 | async-start | bytes 2097152
  818.9 22.8 %slice-start.3 = ((s8[5242880]{0:T(1024)(128)(4,1)}), s8[4194304]{0:T(1024)(128)(4,1)S(1)}, s32[]{:S(2)}) async-start(s8[5242880]{0:T(1024)(128)(4,1)} %bitcast.53), calls=%async_computation.7 | async-start | bytes 8388608
Sparse Core Ops, SparseCore 0:
  9.1 89.1 all-gather.7
  106.9 210.2 all-gather.9
  348.0 215.3 all-gather.11
  603.3 215.5 all-gather.13
